TPU v7x, 32 devices: a whole 2x2x4 slice. The times are simulated.
32 devices in a mesh: grp: 8 (over z, core), tp: 4 (over y, x).
Axes of the slice: x: 2, y: 2, z: 4, core: 2. Of those that a mesh axis runs over, the one named last changes fastest.
Arguments:
- stream: bfloat16 [2048, 2048], P(('grp', 'tp')), may hold values from -6 to 6
- lengths: int32 [6], replicated, may hold values from 1 to 1024, 2048 in all
- att_routes: int32 [2048, 2], P(('grp', 'tp')), may hold values from 0 to 7, all different within a row
- att_gate: bfloat16 [2048, 2], P(('grp', 'tp')), may hold values from 0.19921875 to 1
- mlp_routes: int32 [2048, 2], P(('grp', 'tp')), may hold values from 0 to 7, all different within a row; in each aligned block of 256 rows (0 to 255, 256 to 511, ...) at most 80 rows name the same one
- mlp_gate: bfloat16 [2048, 2], P(('grp', 'tp')), may hold values from 0.19921875 to 1
- gain_attn: float32 [2048], replicated, may hold values from 0.25 to 1.75
- gain_mlp: float32 [2048], replicated, may hold values from 0.25 to 1.75
- w_query: bfloat16 [8, 2048, 2048], P(None, None, 'tp')
- w_key: bfloat16 [2048, 2048], P(None, 'tp')
- w_value: bfloat16 [2048, 2048], P(None, 'tp'), may hold values from -0.125 to 0.125
- w_output: bfloat16 [8, 2048, 2048], P(None, 'tp'), may hold values from -0.125 to 0.125
- w_gate: bfloat16 [2048, 45056], P(None, ('grp', 'tp')), may hold values from -0.125 to 0.125
- w_up: bfloat16 [2048, 45056], P(None, ('grp', 'tp')), may hold values from -0.125 to 0.125
- w_down: bfloat16 [45056, 2048], P(('grp', 'tp')), may hold values from -0.078125 to 0.078125
- cache_in: bfloat16 [2048, 4, 2, 16, 128], P('grp', None, None, 'tp'), may hold values from -6 to 6
- page_table: int32 [128], P('grp'), may hold values from 0 to 127, as said below
Outputs:
- hidden_out: bfloat16 [2048, 2048], P('grp', 'tp')
- cache_out: bfloat16 [128, 16, 4, 2, 16, 128], P('grp', None, None, None, 'tp')
Inputs may be any that keep to these rules, and one draw needn't show every extreme that they name: Request r takes the lengths[r] tokens after those of requests 0 to r - 1; they sum to 2048 and the longest has exactly 1024. `att_routes`: the 2 experts of a token differ. `mlp_routes`: the 2 experts of a token differ; in each aligned block of 256 rows no expert is named by more than 80 rows, a bound that some block reaches. `page_table`: a permutation; of the 16 pages of each aligned block of 16 pages, exactly 2 go to each aligned block of 16 slots.
All inputs are finite; a program needn't handle non-finite values.
Results may differ from a plain program's by a relative error of at most 0.014.
Values may be sent and summed in bfloat16 or wider, within the bound.
A program may use at most 192 MiB of HBM per device.

v0:
```python
import functools

import jax
import jax.numpy as jnp
from jax import lax
from jax.experimental import pallas as pl
from jax.experimental.pallas import tpu as pltpu
from jax.sharding import PartitionSpec as P

HD = 128
E_ATT = 8
E_MLP = 8
TOPK = 2
META = 128
MESH = pl.DeviceIdType.MESH
VMEM_LIMIT = 56 * 1024 * 1024


epsilon = 1e-06
rope_base = 10000.0
masked_score = -1e30

ANY = pl.BlockSpec(memory_space=pl.ANY)
VM = pl.BlockSpec(memory_space=pltpu.VMEM)


def params(collective=None):
    if collective is None:
        return pltpu.CompilerParams(vmem_limit_bytes=VMEM_LIMIT)
    return pltpu.CompilerParams(
        vmem_limit_bytes=VMEM_LIMIT, collective_id=collective, has_side_effects=True
    )


def turn_heads(values, cosine, sine, heads):
    parts = []
    for head in range(heads):
        part = values[:, head * HD : (head + 1) * HD]
        parts.append(part * cosine + pltpu.roll(part, HD // 2, 1) * sine)
    return jnp.concatenate(parts, axis=1)


def key_value_kernel(
    tp_count, stream, meta, gain, cosine, sine, w_key, w_value,
    normed, kvm, resid,
    rows_all, meta_all, wk, wv, wsem, send, recv, msend, mrecv,
):
    tp = lax.axis_index("tp")
    rows = stream.shape[0]
    width = wk.shape[1]
    load_k = pltpu.make_async_copy(w_key, wk, wsem.at[0])
    load_v = pltpu.make_async_copy(w_value, wv, wsem.at[1])
    load_k.start()
    load_v.start()
    barrier = pltpu.get_barrier_semaphore()
    for j in range(1, tp_count):
        pl.semaphore_signal(
            barrier, inc=1, device_id={"tp": (tp + j) % tp_count}, device_id_type=MESH
        )
    mine = pl.ds(pl.multiple_of(tp * rows, rows), rows)
    pl.semaphore_wait(barrier, tp_count - 1)
    copies = []
    for j in range(1, tp_count):
        peer = {"tp": (tp + j) % tp_count}
        copies.append(
            pltpu.make_async_remote_copy(
                stream, rows_all.at[mine], send.at[j - 1], recv.at[j - 1], peer, MESH
            )
        )
        copies.append(
            pltpu.make_async_remote_copy(
                meta, meta_all.at[mine], msend.at[j - 1], mrecv.at[j - 1], peer, MESH
            )
        )
    for copy in copies:
        copy.start()
    rows_all[mine, :] = stream[...]
    meta_all[mine, :] = meta[...]
    for copy in copies:
        copy.wait()
    widened = rows_all[...].astype(jnp.float32)
    mean_square = jnp.mean(widened * widened, axis=-1, keepdims=True)
    hidden = (widened * lax.rsqrt(mean_square + epsilon) * gain[...]).astype(jnp.bfloat16)
    normed[...] = hidden
    resid[...] = rows_all[:, pl.ds(pl.multiple_of(tp * width, 128), width)]
    kvm[:, 2 * width :] = meta_all[...]
    load_k.wait()
    keys = jnp.dot(hidden, wk[...], preferred_element_type=jnp.float32)
    kvm[:, :width] = turn_heads(keys, cosine[...], sine[...], width // HD).astype(jnp.bfloat16)
    load_v.wait()
    values = jnp.dot(hidden, wv[...], preferred_element_type=jnp.float32)
    kvm[:, width : 2 * width] = values.astype(jnp.bfloat16)


def query_kernel(normed, meta, cosine, sine, w_query, query, total):
    expert = pl.program_id(0)
    width = w_query.shape[2]

    @pl.when(expert == 0)
    def _():
        total[...] = jnp.zeros_like(total)

    projected = jnp.dot(normed[...], w_query[0], preferred_element_type=jnp.float32)
    ids = meta[...].astype(jnp.float32)
    wanted = expert.astype(jnp.float32)
    for k in range(TOPK):
        total[k] = jnp.where(ids[:, k : k + 1] == wanted, projected, total[k])

    @pl.when(expert == E_ATT - 1)
    def _():
        for k in range(TOPK):
            query[k] = turn_heads(total[k], cosine[...], sine[...], width // HD).astype(
                jnp.bfloat16
            )


def attend_kernel(
    tp_count, grp_count, query, starts, meta, resid, kv_all, w_out,
    middle,
    kv, wo, att, mixed, outgoing, incoming, kvsem, wsem, send, recv,
):
    tp = lax.axis_index("tp")
    grp = lax.axis_index("grp")
    tok, width = resid.shape
    window = kv.shape[0]
    reach = grp_count // 2
    base = (grp // reach) * (grp - reach)
    load_kv = pltpu.make_async_copy(
        kv_all.at[pl.ds(pl.multiple_of(base * tok, tok), window), pl.ds(0, 2 * width)],
        kv, kvsem.at[0],
    )
    load_kv.start()
    load_w = [
        pltpu.make_async_copy(w_out.at[e], wo.at[pl.ds(e * width, width)], wsem.at[e])
        for e in range(E_ATT)
    ]
    for load in load_w:
        load.start()
    barrier = pltpu.get_barrier_semaphore()
    for j in range(1, tp_count):
        pl.semaphore_signal(
            barrier, inc=1, device_id={"tp": (tp + j) % tp_count}, device_id_type=MESH
        )
    column = lax.broadcasted_iota(jnp.int32, (tok, window), 1) + base * tok
    row = lax.broadcasted_iota(jnp.int32, (tok, window), 0) + grp * tok
    live = (column <= row) & (column >= starts[...])
    bias = jnp.where(live, 0.0, masked_score)
    load_kv.wait()
    scale = HD ** (-0.5)
    for head in range(width // HD):
        lanes = slice(head * HD, (head + 1) * HD)
        key_head = kv[:, lanes]
        value_head = kv[:, width + head * HD : width + (head + 1) * HD]
        for k in range(TOPK):
            scores = lax.dot_general(
                query[k, :, lanes], key_head, (((1,), (1,)), ((), ())),
                preferred_element_type=jnp.float32,
            ) + bias
            top = jnp.max(scores, axis=-1, keepdims=True)
            weights = jnp.exp((scores - top) * scale)
            total = jnp.sum(weights, axis=-1, keepdims=True)
            summed = jnp.dot(
                weights.astype(jnp.bfloat16), value_head, preferred_element_type=jnp.float32
            )
            att[k, :, lanes] = summed / total
    info = meta[...].astype(jnp.float32)
    for e in range(E_ATT):
        mix = None
        for k in range(TOPK):
            gate = jnp.where(info[:, k : k + 1] == float(e), info[:, TOPK + k : TOPK + k + 1], 0.0)
            term = gate * att[k]
            mix = term if mix is None else mix + term
        mixed[:, e * width : (e + 1) * width] = mix.astype(jnp.bfloat16)
    for load in load_w:
        load.wait()
    pl.semaphore_wait(barrier, tp_count - 1)
    copies = []
    for j in list(range(1, tp_count)) + [0]:
        peer = (tp + j) % tp_count
        part = jnp.dot(
            mixed[...], wo[:, pl.ds(pl.multiple_of(peer * width, 128), width)],
            preferred_element_type=jnp.float32,
        )
        if j:
            outgoing[j - 1] = part.astype(jnp.bfloat16)
            copy = pltpu.make_async_remote_copy(
                outgoing.at[j - 1], incoming.at[j - 1], send.at[j - 1], recv.at[j - 1],
                {"tp": peer}, MESH,
            )
            copy.start()
            copies.append(copy)
    result = resid[...].astype(jnp.float32) + part
    for j, copy in enumerate(copies):
        copy.wait()
        result = result + incoming[j].astype(jnp.float32)
    middle[...] = result.astype(jnp.bfloat16)


def expert_kernel(
    tp_count, grp_count, cap, step_blocks,
    mid_all, select, mid, mix, gain, w_gate, w_up, w_down, pages,
    out, arrived,
    wg, wu, wd, gathered, xn, rs_own, rs_out, rs_in, ret_out, ret_in,
    wsem, self_sem, psend, precv, asend, arecv, rsend, rrecv, tsend, trecv,
):
    tp = lax.axis_index("tp")
    grp = lax.axis_index("grp")
    width = mid.shape[1]
    loads = [
        pltpu.make_async_copy(src, dst, wsem.at[i])
        for i, (src, dst) in enumerate(((w_gate, wg), (w_up, wu), (w_down, wd)))
    ]
    for load in loads:
        load.start()
    barrier = pltpu.get_barrier_semaphore()
    for j in range(1, tp_count):
        pl.semaphore_signal(
            barrier, inc=1, device_id={"tp": (tp + j) % tp_count}, device_id_type=MESH
        )
    for j in range(1, grp_count):
        pl.semaphore_signal(
            barrier, inc=1, device_id={"grp": (grp + j) % grp_count}, device_id_type=MESH
        )
    self_copy = pltpu.make_async_copy(pages.at[grp], arrived.at[grp], self_sem.at[0])
    self_copy.start()

    step_rows = step_blocks * cap
    steps = grp_count // step_blocks

    def pick(step):
        for i in range(step * step_blocks, (step + 1) * step_blocks):
            block = (grp + 1 + i) % grp_count
            rows = jnp.dot(select[block], mid_all[block], preferred_element_type=jnp.float32)
            gathered[tp, i * cap : (i + 1) * cap, :] = rows.astype(jnp.bfloat16)

    ag = []

    def spread(step):
        rows = pl.ds(step * step_rows, step_rows)
        ag.append([])
        for j in range(1, tp_count):
            copy = pltpu.make_async_remote_copy(
                gathered.at[tp, rows], gathered.at[tp, rows],
                asend.at[step, j - 1], arecv.at[step, j - 1],
                {"tp": (tp + j) % tp_count}, MESH,
            )
            copy.start()
            ag[step].append(copy)

    pick(0)
    pl.semaphore_wait(barrier, tp_count - 1 + grp_count - 1)
    spread(0)
    page_copies = []
    for j in range(1, grp_count):
        peer = (grp + j) % grp_count
        copy = pltpu.make_async_remote_copy(
            pages.at[peer], arrived.at[grp], psend.at[j - 1], precv.at[j - 1],
            {"grp": peer}, MESH,
        )
        copy.start()
        page_copies.append(copy)
    for step in range(1, steps):
        pick(step)
        spread(step)
    for load in loads:
        load.wait()

    rs = []
    ret = []

    def give_back(step):
        rows = slice(step * step_rows, (step + 1) * step_rows)
        total = rs_own[rows, :]
        for j in range(tp_count - 1):
            rs[step][j].wait_recv()
            total = total + rs_in[j, rows, :].astype(jnp.float32)
        ret_out[rows, :] = total.astype(jnp.bfloat16)
        for i in range(step * step_blocks, (step + 1) * step_blocks):
            part = slice(i * cap, (i + 1) * cap)
            mine = pl.ds(pl.multiple_of(grp * cap, cap), cap)
            if i == grp_count - 1:
                ret_in[mine, :] = ret_out[part, :]
            else:
                copy = pltpu.make_async_remote_copy(
                    ret_out.at[pl.ds(i * cap, cap)], ret_in.at[mine],
                    tsend.at[i], trecv.at[i],
                    {"grp": (grp + 1 + i) % grp_count}, MESH,
                )
                copy.start()
                ret.append(copy)

    for step in range(steps):
        rows = slice(step * step_rows, (step + 1) * step_rows)
        for copy in ag[step]:
            copy.wait_recv()
        square = None
        for s in range(tp_count):
            part = gathered[s, rows, :].astype(jnp.float32)
            term = jnp.sum(part * part, axis=-1, keepdims=True)
            square = term if square is None else square + term
        factor = lax.rsqrt(square * (1.0 / (tp_count * width)) + epsilon)
        for s in range(tp_count):
            lanes = slice(s * width, (s + 1) * width)
            xn[:, lanes] = (
                gathered[s, rows, :].astype(jnp.float32) * factor * gain[:, lanes]
            ).astype(jnp.bfloat16)
        gate = jnp.dot(xn[...], wg[...], preferred_element_type=jnp.float32)
        up = jnp.dot(xn[...], wu[...], preferred_element_type=jnp.float32)
        hidden = (gate / (1.0 + jnp.exp(-gate)) * up).astype(jnp.bfloat16)
        rs.append([])
        for j in list(range(1, tp_count)) + [0]:
            peer = (tp + j) % tp_count
            part = jnp.dot(
                hidden, wd[:, pl.ds(pl.multiple_of(peer * width, 128), width)],
                preferred_element_type=jnp.float32,
            )
            if j:
                rs_out[j - 1, rows, :] = part.astype(jnp.bfloat16)
                span = pl.ds(step * step_rows, step_rows)
                copy = pltpu.make_async_remote_copy(
                    rs_out.at[j - 1, span], rs_in.at[j - 1, span],
                    rsend.at[step, j - 1], rrecv.at[step, j - 1],
                    {"tp": peer}, MESH,
                )
                copy.start()
                rs[step].append(copy)
            else:
                rs_own[rows, :] = part
        if step:
            give_back(step - 1)
    give_back(steps - 1)
    for copy in ret:
        copy.wait()
    for group in ag + rs:
        for copy in group:
            copy.wait_send()
    out[...] = (
        mid[...].astype(jnp.float32)
        + jnp.dot(mix[...], ret_in[...], preferred_element_type=jnp.float32)
    ).astype(jnp.bfloat16)
    self_copy.wait()
    for copy in page_copies:
        copy.wait()


def pick_pages_kernel(order, pages, picked, sem):
    count = pages.shape[0]
    copies = [
        pltpu.make_async_copy(pages.at[order[i]], picked.at[i], sem.at[i]) for i in range(count)
    ]
    for copy in copies:
        copy.start()
    for copy in copies:
        copy.wait()


def on_device(
    stream,
    lengths,
    att_routes,
    att_gate,
    mlp_routes,
    mlp_gate,
    gain_attn,
    gain_mlp,
    w_query,
    w_key,
    w_value,
    w_output,
    w_gate,
    w_up,
    w_down,
    cache_in,
    page_table,
):
    grp_count = lax.axis_size("grp")
    tp_count = lax.axis_size("tp")
    grp_index = lax.axis_index("grp")
    rows, model_width = stream.shape
    tok = rows * tp_count
    total_tok = tok * grp_count
    width = w_key.shape[1]
    pages_dev = page_table.shape[0]
    bf16 = jnp.bfloat16
    f32 = jnp.float32
    dma = pltpu.SemaphoreType.DMA
    sds = jax.ShapeDtypeStruct

    query_index = grp_index * tok + jnp.arange(tok, dtype=jnp.int32)
    ends = jnp.sum(
        jnp.where(
            jnp.arange(lengths.shape[0])[None, :] <= jnp.arange(lengths.shape[0])[:, None],
            lengths[None, :], 0,
        ),
        axis=1,
    )
    passed = ends[None, :] <= query_index[:, None]
    starts = jnp.max(jnp.where(passed, ends[None, :], 0), axis=1, keepdims=True)
    position = (query_index[:, None] - starts).astype(f32)
    frequency = rope_base ** (-(jnp.arange(HD // 2, dtype=f32) * 2.0 / HD))
    angles = position * frequency[None, :]
    cos_half, sin_half = jnp.cos(angles), jnp.sin(angles)
    cosine = jnp.concatenate([cos_half, cos_half], axis=1)
    sine = jnp.concatenate([-sin_half, sin_half], axis=1)

    meta = jnp.concatenate(
        [
            att_routes.astype(bf16),
            att_gate,
            mlp_routes.astype(bf16),
            mlp_gate,
            jnp.broadcast_to(page_table.astype(bf16)[None, :], (rows, pages_dev)),
        ],
        axis=1,
    )
    meta = jnp.pad(meta, ((0, 0), (0, META - meta.shape[1])))

    normed, kvm, resid = pl.pallas_call(
        functools.partial(key_value_kernel, tp_count),
        out_shape=(
            sds((tok, model_width), bf16),
            sds((tok, 2 * width + META), bf16),
            sds((tok, width), bf16),
        ),
        in_specs=[VM] * 5 + [ANY] * 2,
        out_specs=(VM,) * 3,
        scratch_shapes=[
            pltpu.VMEM((tok, model_width), bf16),
            pltpu.VMEM((tok, META), bf16),
            pltpu.VMEM(w_key.shape, bf16),
            pltpu.VMEM(w_value.shape, bf16),
            dma((2,)),
            dma((tp_count - 1,)),
            dma((tp_count - 1,)),
            dma((tp_count - 1,)),
            dma((tp_count - 1,)),
        ],
        compiler_params=params(1),
        name="gather_key_value",
    )(stream, meta, gain_attn[None, :], cosine, sine, w_key, w_value)

    kv_all = lax.all_gather(kvm, "grp", axis=0, tiled=True)

    meta_block = 2 * width // META
    query = pl.pallas_call(
        query_kernel,
        grid=(E_ATT,),
        out_shape=sds((TOPK, tok, width), bf16),
        in_specs=[
            pl.BlockSpec((tok, model_width), lambda e: (0, 0)),
            pl.BlockSpec((tok, META), lambda e: (0, meta_block)),
            pl.BlockSpec((tok, HD), lambda e: (0, 0)),
            pl.BlockSpec((tok, HD), lambda e: (0, 0)),
            pl.BlockSpec((1, model_width, width), lambda e: (e, 0, 0)),
        ],
        out_specs=pl.BlockSpec((TOPK, tok, width), lambda e: (0, 0, 0)),
        scratch_shapes=[pltpu.VMEM((TOPK, tok, width), f32)],
        compiler_params=params(),
        name="query",
    )(normed, kvm, cosine, sine, w_query)

    info = kvm[:, 2 * width :]
    window = (grp_count // 2 + 1) * tok
    middle = pl.pallas_call(
        functools.partial(attend_kernel, tp_count, grp_count),
        out_shape=sds((tok, width), bf16),
        in_specs=[VM] * 4 + [ANY] * 2,
        out_specs=VM,
        scratch_shapes=[
            pltpu.VMEM((window, 2 * width), bf16),
            pltpu.VMEM((E_ATT * width, model_width), bf16),
            pltpu.VMEM((TOPK, tok, width), f32),
            pltpu.VMEM((tok, E_ATT * width), bf16),
            pltpu.VMEM((tp_count - 1, tok, width), bf16),
            pltpu.VMEM((tp_count - 1, tok, width), bf16),
            dma((1,)),
            dma((E_ATT,)),
            dma((tp_count - 1,)),
            dma((tp_count - 1,)),
        ],
        compiler_params=params(2),
        name="attend",
    )(query, starts, info, resid, kv_all, w_output)

    mid_all = lax.all_gather(middle, "grp", axis=0, tiled=False)

    capacity = tok * TOPK * 5 // (E_MLP * 4)
    per_owner = grp_count // E_MLP
    my_expert = (grp_index // per_owner).astype(f32)
    meta_all = kv_all[:, 2 * width :].reshape(grp_count, tok, META)
    lower = jnp.arange(tok)[:, None] < jnp.arange(tok)[None, :]
    lower = lower.astype(bf16)
    hit = jnp.any(meta_all[:, :, 4:6].astype(f32) == my_expert, axis=2)
    rank = jnp.dot(hit.astype(bf16), lower, preferred_element_type=f32).astype(jnp.int32)
    slot_ids = jnp.arange(capacity, dtype=jnp.int32)
    select = (
        hit[:, None, :] & (rank[:, None, :] == slot_ids[None, :, None])
    ).astype(bf16)
    own_ids = info[:, 4:6].astype(jnp.int32)
    own_gate = info[:, 6:8].astype(f32)
    owner_expert = jnp.arange(grp_count, dtype=jnp.int32) // per_owner
    own_hot = own_ids[:, :, None] == owner_expert[None, None, :]
    own_weight = jnp.sum(jnp.where(own_hot, own_gate[:, :, None], 0.0), axis=1)
    own_hit = jnp.any(own_hot, axis=1)
    own_rank = jnp.dot(lower.T, own_hit.astype(bf16), preferred_element_type=f32).astype(jnp.int32)
    mix = jnp.where(
        own_rank[:, :, None] == slot_ids[None, None, :], own_weight[:, :, None], 0.0
    ).astype(bf16).reshape(tok, grp_count * capacity)

    page_len = tok // pages_dev
    pair_pages = pages_dev // grp_count
    page_blocks = cache_in.reshape((pages_dev, page_len) + cache_in.shape[1:])
    page_ids = jnp.arange(pages_dev, dtype=jnp.int32)
    sort_key = (page_table // pages_dev) * pages_dev + page_ids
    place = jnp.sum((sort_key[None, :] < sort_key[:, None]).astype(jnp.int32), axis=1)
    page_order = jnp.sum(
        jnp.where(place[None, :] == page_ids[:, None], page_ids[None, :], 0), axis=1
    )
    move_pages = pl.pallas_call(
        pick_pages_kernel,
        out_shape=sds(page_blocks.shape, bf16),
        in_specs=[pl.BlockSpec(memory_space=pltpu.SMEM), ANY],
        out_specs=ANY,
        scratch_shapes=[dma((pages_dev,))],
        compiler_params=pltpu.CompilerParams(),
        name="pick_pages",
    )
    page_sends = move_pages(page_order, page_blocks).reshape(
        (grp_count, pair_pages) + page_blocks.shape[1:]
    )

    hid = w_gate.shape[1]
    step_blocks = 2
    steps = grp_count // step_blocks
    slots = grp_count * capacity
    peers = tp_count - 1
    hidden_out, arrived = pl.pallas_call(
        functools.partial(expert_kernel, tp_count, grp_count, capacity, step_blocks),
        out_shape=(sds((tok, width), bf16), sds(page_sends.shape, bf16)),
        in_specs=[VM] * 5 + [ANY] * 4,
        out_specs=(VM, ANY),
        scratch_shapes=[
            pltpu.VMEM((model_width, hid), bf16),
            pltpu.VMEM((model_width, hid), bf16),
            pltpu.VMEM((hid, model_width), bf16),
            pltpu.VMEM((tp_count, slots, width), bf16),
            pltpu.VMEM((step_blocks * capacity, model_width), bf16),
            pltpu.VMEM((slots, width), f32),
            pltpu.VMEM((peers, slots, width), bf16),
            pltpu.VMEM((peers, slots, width), bf16),
            pltpu.VMEM((slots, width), bf16),
            pltpu.VMEM((slots, width), bf16),
            dma((3,)),
            dma((1,)),
            dma((grp_count - 1,)),
            dma((grp_count - 1,)),
            dma((steps, peers)),
            dma((steps, peers)),
            dma((steps, peers)),
            dma((steps, peers)),
            dma((grp_count - 1,)),
            dma((grp_count - 1,)),
        ],
        compiler_params=params(3),
        name="experts",
    )(mid_all, select, middle, mix, gain_mlp[None, :], w_gate, w_up, w_down, page_sends)

    tables = meta_all[:, 0, 8 : 8 + pages_dev].astype(jnp.int32).reshape(-1)
    here = tables // pages_dev == grp_index
    all_ids = jnp.arange(tables.shape[0], dtype=jnp.int32)
    arrival = jnp.sum(
        (here[None, :] & (all_ids[None, :] < all_ids[:, None])).astype(jnp.int32), axis=1
    )
    local = tables % pages_dev
    slot_source = jnp.sum(
        jnp.where(here[None, :] & (local[None, :] == page_ids[:, None]), arrival[None, :], 0),
        axis=1,
    )
    cache_out = move_pages(slot_source, arrived.reshape(page_blocks.shape))
    return (hidden_out, cache_out)


def solution(mesh):
    return jax.shard_map(
        on_device,
        mesh=mesh,
        in_specs=(
            P(("grp", "tp"), None),
            P(),
            P(("grp", "tp"), None),
            P(("grp", "tp"), None),
            P(("grp", "tp"), None),
            P(("grp", "tp"), None),
            P(),
            P(),
            P(None, None, "tp"),
            P(None, "tp"),
            P(None, "tp"),
            P(None, "tp", None),
            P(None, ("grp", "tp")),
            P(None, ("grp", "tp")),
            P(("grp", "tp"), None),
            P("grp", None, None, "tp", None),
            P("grp"),
        ),
        out_specs=(P("grp", "tp"), P("grp", None, None, None, "tp", None)),
        check_vma=False,
    )
```

profile of v0, /device:TPU:1, one launch (start us, length us, event | category | flops | bytes accessed | tf_op | source)
XLA Modules:
  0.0 330.5 jit_solution(12522067050380276095)
XLA Ops:
  7.2 0.8 select_reduce_fusion.4
  8.0 0.7 convert_element_type.67
  8.7 0.7 convert_element_type.68
  9.5 0.7 iota_add_fusion.1
  10.3 0.7 concatenate.9
  11.0 0.1 copy.45
  11.1 0.6 pad.4.meta
  11.7 0.5 fusion.4
  12.3 0.8 pad_maximum_fusion
  13.1 20.5 %gather_key_value.1 = (bf16[256,2048]{1,0:T(8,128)(2,1)}, bf16[256,1152]{1,0:T(8,128)(2,1)}, bf16[256,512]{1,0:T(8,128)(2,1)}) custom-call(bf16[64,2048]{1,0:T(8,128)(2,1)} %stream.1, bf16[64,128]{1,0:T(8,128)(2,1)} %pad.4.meta, f32[1,2048]{1,0:T(1,128)} %bitcast.24, f32[256,128]{1,0:T(8,128)} %get-tuple-element.19.cosine, ...), custom_call_target="tpu_custom_call" | custom-call | tf_op jit(solution)/shard_map/gather_key_value/pallas_call | solution.py:418
  33.7 1.5 slice.20.meta
  35.1 0.8 copy.46.starts
  35.9 12.1 %query.1 = bf16[2,256,512]{2,1,0:T(8,128)(2,1)} custom-call(bf16[256,2048]{1,0:T(8,128)(2,1)} %get-tuple-element.7.normed, bf16[256,1152]{1,0:T(8,128)(2,1)} %get-tuple-element.8.meta, f32[256,128]{1,0:T(8,128)} %get-tuple-element.19.cosine, f32[256,128]{1,0:T(8,128)} %get-tuple-element.20.sine, bf16[8,2048,512]{2,1,0:T(8,128)(2,1)} %w_query.1), custom_call_target="tpu_custom_call" | custom-call | tf_op jit(solution)/shard_map/query/pallas_call | solution.py:445
  48.1 38.8 %all-gather.4.cloned.1.call-done.kv_all = bf16[2048,1152]{1,0:T(8,128)(2,1)} async-done(((bf16[256,1152]{1,0:T(8,128)(2,1)}), bf16[2048,1152]{1,0:T(8,128)(2,1)}) %all-gather.4.cloned.1.call-update) | async-done | bytes 4718608 | tf_op jit(solution)/shard_map/all_gather | solution.py:442
  86.9 30.5 %attend.1.mid = bf16[256,512]{1,0:T(8,128)(2,1)} custom-call(bf16[2,256,512]{2,1,0:T(8,128)(2,1)} %query.1, s32[256,1]{1,0:T(8,128)} %copy.46.starts, bf16[256,128]{1,0:T(8,128)(2,1)} %slice.20.meta, bf16[256,512]{1,0:T(8,128)(2,1)} %get-tuple-element.9.resid, bf16[2048,1152]{1,0:T(8,128)(2,1)} %all-gather.4.cloned.1.call-done.kv_all, ...), custom_call_target="tpu_custom_call" | custom-call | tf_op jit(solution)/shard_map/attend/pallas_call | solution.py:464
  117.5 1.0 slice_convert_fusion.1
  118.8 0.2 copy.50
  119.0 0.1 convolution_convert_fusion
  119.2 0.2 copy.48
  119.4 0.2 convert_reduce_fusion.1
  119.6 0.6 select_reduce_fusion.2.order
  120.3 65.4 %pick_pages.2 = bf16[16,16,4,2,4,128]{5,4,3,2,1,0:T(4,128)(2,1)} custom-call(s32[16]{0:T(128)} %select_reduce_fusion.2.order, bf16[16,16,4,2,4,128]{5,4,3,2,1,0:T(4,128)(2,1)} %bitcast.19), custom_call_target="tpu_custom_call" | custom-call | tf_op jit(solution)/shard_map/pick_pages/pallas_call | solution.py:528
  185.7 0.8 select_convert_fusion.mix
  186.5 1.1 slice.26
  187.8 0.1 convert_reduce_fusion
  187.9 0.6 select_reduce_fusion.1.order
  188.5 0.5 fusion
  189.1 0.1 convolution_convert_fusion.1
  189.2 0.9 fusion.2.select
  190.1 67.2 %experts.1 = (bf16[256,512]{1,0:T(8,128)(2,1)}, bf16[8,2,16,4,2,4,128]{6,5,4,3,2,1,0:T(4,128)(2,1)}) custom-call(bf16[8,256,512]{2,1,0:T(8,128)(2,1)} %bitcast.18, bf16[8,80,256]{2,1,0:T(8,128)(2,1)} %fusion.2.select, bf16[256,512]{1,0:T(8,128)(2,1)} %attend.1.mid, bf16[256,640]{1,0:T(8,128)(2,1)} %select_convert_fusion.mix, f32[1,2048]{1,0:T(1,128)} %bitcast.23, ...), custom_call_target="tpu_custom_call" | custom-call | tf_op jit(solution)/shard_map/experts/pallas_call | solution.py:537
  257.4 65.6 %pick_pages.3 = bf16[16,16,4,2,4,128]{5,4,3,2,1,0:T(4,128)(2,1)} custom-call(s32[16]{0:T(128)} %select_reduce_fusion.1.order, bf16[16,16,4,2,4,128]{5,4,3,2,1,0:T(4,128)(2,1)} %bitcast.20), custom_call_target="tpu_custom_call" | custom-call | tf_op jit(solution)/shard_map/pick_pages/pallas_call | solution.py:579
  323.0 0.7 copy.55
  (25 shorter events, 0.8 us)
Async XLA Ops:
  7.2 79.7 %all-gather.4.cloned.1.call-start = ((), (), s32[]{:S(2)}) async-start(), calls=%async_computation | async-start | bytes 5308416 | tf_op jit(solution)/shard_map/all_gather | solution.py:442
  33.6 156.5 %all-gather.6.cloned.1.call-start = ((), (), s32[]{:S(2)}) async-start(), calls=%async_computation.1 | async-start | bytes 2359296 | tf_op jit(solution)/shard_map/all_gather | solution.py:485
  257.4 65.6 %copy-start = (bf16[256,512]{1,0:T(8,128)(2,1)S(1)}, bf16[256,512]{1,0:T(8,128)(2,1)}, u32[]{:S(2)}) copy-start(bf16[256,512]{1,0:T(8,128)(2,1)} %get-tuple-element.23) | copy-start | bytes 786436
Sparse Core Ops, SparseCore 0:
  33.7 53.1 all-gather.3
  117.6 27.4 all-gather.5
where the time goes:
time: 331 us
  Pallas kernels  261 us (79%)
  waiting for transfers between devices  38.9 us (12%)
  between operations  14.2 us (4%)
  other arithmetic  9.22 us (3%)
  local copies, waits for them, and re-layouts  6.47 us (2%)
    pallas_call x1, Pallas kernels, on_device(): pl.pallas_call(functools.partial(expert_kernel, tp_count, grp_count, capa...  67.2 us
    pallas_call x1, Pallas kernels, on_device(): cache_out = move_pages(slot_source, arrived.reshape(page_blocks.shape))  65.6 us
    pallas_call x1, Pallas kernels, on_device(): move_pages(page_order, page_blocks)  65.4 us
    all_gather x1, waiting for transfers between devices, on_device(): kv_all = lax.all_gather(kvm, 'grp', axis=0, tiled=True)  38.8 us
    pallas_call x1, Pallas kernels, on_device(): pl.pallas_call(functools.partial(attend_kernel, tp_count, grp_count), out...  30.5 us
    pallas_call x1, Pallas kernels, on_device(): pl.pallas_call(functools.partial(key_value_kernel, tp_count), out_shape=(...  20.5 us
    pallas_call x1, Pallas kernels, on_device(): pl.pallas_call(query_kernel, grid=(E_ATT,), out_shape=sds((TOPK, tok, wid...  12.1 us
  transfers between devices with their start and end apart: 2, of which 1 were waited for; matrix products, arithmetic and copies ran while one was open for 3% of the time, Pallas kernels for 23%

commit v1 on v0

--- a/solution.py
+++ b/solution.py
@@ -42,8 +42,8 @@
 
 def key_value_kernel(
     tp_count, stream, meta, gain, cosine, sine, w_key, w_value,
-    normed, kvm, resid,
-    rows_all, meta_all, wk, wv, wsem, send, recv, msend, mrecv,
+    normed, kvm, info, resid,
+    rows_all, wk, wv, wsem, send, recv, msend, mrecv,
 ):
     tp = lax.axis_index("tp")
     rows = stream.shape[0]
@@ -69,13 +69,13 @@
         )
         copies.append(
             pltpu.make_async_remote_copy(
-                meta, meta_all.at[mine], msend.at[j - 1], mrecv.at[j - 1], peer, MESH
+                meta, info.at[mine], msend.at[j - 1], mrecv.at[j - 1], peer, MESH
             )
         )
     for copy in copies:
         copy.start()
     rows_all[mine, :] = stream[...]
-    meta_all[mine, :] = meta[...]
+    info[mine, :] = meta[...]
     for copy in copies:
         copy.wait()
     widened = rows_all[...].astype(jnp.float32)
@@ -83,7 +83,6 @@
     hidden = (widened * lax.rsqrt(mean_square + epsilon) * gain[...]).astype(jnp.bfloat16)
     normed[...] = hidden
     resid[...] = rows_all[:, pl.ds(pl.multiple_of(tp * width, 128), width)]
-    kvm[:, 2 * width :] = meta_all[...]
     load_k.wait()
     keys = jnp.dot(hidden, wk[...], preferred_element_type=jnp.float32)
     kvm[:, :width] = turn_heads(keys, cosine[...], sine[...], width // HD).astype(jnp.bfloat16)
@@ -92,65 +91,115 @@
     kvm[:, width : 2 * width] = values.astype(jnp.bfloat16)
 
 
-def query_kernel(normed, meta, cosine, sine, w_query, query, total):
-    expert = pl.program_id(0)
-    width = w_query.shape[2]
-
-    @pl.when(expert == 0)
-    def _():
-        total[...] = jnp.zeros_like(total)
-
-    projected = jnp.dot(normed[...], w_query[0], preferred_element_type=jnp.float32)
-    ids = meta[...].astype(jnp.float32)
-    wanted = expert.astype(jnp.float32)
-    for k in range(TOPK):
-        total[k] = jnp.where(ids[:, k : k + 1] == wanted, projected, total[k])
-
-    @pl.when(expert == E_ATT - 1)
-    def _():
-        for k in range(TOPK):
-            query[k] = turn_heads(total[k], cosine[...], sine[...], width // HD).astype(
-                jnp.bfloat16
-            )
+def send_pages(grp_count, half, pages, arrived, self_sem, psend, precv):
+    grp = lax.axis_index("grp")
+    copies = [pltpu.make_async_copy(pages.at[grp, half], arrived.at[grp], self_sem.at[0])]
+    for j in range(1, grp_count):
+        peer = (grp + j) % grp_count
+        copies.append(
+            pltpu.make_async_remote_copy(
+                pages.at[peer, half], arrived.at[grp], psend.at[j - 1], precv.at[j - 1],
+                {"grp": peer}, MESH,
+            )
+        )
+    for copy in copies:
+        copy.start()
+    return copies
 
 
 def attend_kernel(
-    tp_count, grp_count, query, starts, meta, resid, kv_all, w_out,
-    middle,
-    kv, wo, att, mixed, outgoing, incoming, kvsem, wsem, send, recv,
+    tp_count, grp_count, first,
+    normed, cosine, sine, starts, meta, resid, own_kv, table, w_query, w_out, pages,
+    middle, arrived, tables,
+    wq, wo, kv, total, query, att, mixed, outgoing, incoming,
+    qsem, wsem, ring_send, ring_recv, side_send, side_recv, send, recv,
+    self_sem, psend, precv, tsend, trecv,
 ):
     tp = lax.axis_index("tp")
     grp = lax.axis_index("grp")
+    core = grp % 2
     tok, width = resid.shape
-    window = kv.shape[0]
     reach = grp_count // 2
-    base = (grp // reach) * (grp - reach)
-    load_kv = pltpu.make_async_copy(
-        kv_all.at[pl.ds(pl.multiple_of(base * tok, tok), window), pl.ds(0, 2 * width)],
-        kv, kvsem.at[0],
-    )
-    load_kv.start()
+    window = (reach + 1) * tok
+    load_q = [pltpu.make_async_copy(w_query.at[e], wq.at[e], qsem.at[e]) for e in range(E_ATT)]
     load_w = [
         pltpu.make_async_copy(w_out.at[e], wo.at[pl.ds(e * width, width)], wsem.at[e])
         for e in range(E_ATT)
     ]
-    for load in load_w:
+    for load in load_q + load_w:
         load.start()
     barrier = pltpu.get_barrier_semaphore()
     for j in range(1, tp_count):
         pl.semaphore_signal(
             barrier, inc=1, device_id={"tp": (tp + j) % tp_count}, device_id_type=MESH
         )
-    column = lax.broadcasted_iota(jnp.int32, (tok, window), 1) + base * tok
+    for j in range(1, grp_count):
+        pl.semaphore_signal(
+            barrier, inc=1, device_id={"grp": (grp + j) % grp_count}, device_id_type=MESH
+        )
+    kv[reach] = own_kv[...]
+    pl.semaphore_wait(barrier, tp_count - 1 + grp_count - 1)
+
+    hops = reach // 2
+    onward = {"grp": (grp + 2) % grp_count}
+    other = {"grp": grp + 1 - 2 * core}
+
+    def ring(h):
+        return pltpu.make_async_remote_copy(
+            kv.at[reach - 2 * h], kv.at[reach - 2 * h - 2],
+            ring_send.at[h], ring_recv.at[h], onward, MESH,
+        )
+
+    def side(n):
+        return pltpu.make_async_remote_copy(
+            kv.at[reach - 2 * (core + n)], kv.at[reach - 1 - 2 * n],
+            side_send.at[n], side_recv.at[n], other, MESH,
+        )
+
+    rings = [ring(h) for h in range(hops)]
+    sides = [side(n) for n in range(hops)]
+    rings[0].start()
+
+    table_copies = []
+    for j in range(1, grp_count):
+        table_copies.append(
+            pltpu.make_async_remote_copy(
+                table, tables.at[grp], tsend.at[j - 1], trecv.at[j - 1],
+                {"grp": (grp + j) % grp_count}, MESH,
+            )
+        )
+    for copy in table_copies:
+        copy.start()
+    tables[grp] = table[...]
+
+    ids = meta[...].astype(jnp.float32)
+    total[...] = jnp.zeros_like(total)
+    for e in range(E_ATT):
+        load_q[e].wait()
+        projected = jnp.dot(normed[...], wq[e], preferred_element_type=jnp.float32)
+        for k in range(TOPK):
+            total[k] = jnp.where(
+                ids[:, first + k : first + k + 1] == float(e), projected, total[k]
+            )
+    for k in range(TOPK):
+        query[k] = turn_heads(total[k], cosine[...], sine[...], width // HD).astype(jnp.bfloat16)
+    column = lax.broadcasted_iota(jnp.int32, (tok, window), 1) + (grp - reach) * tok
     row = lax.broadcasted_iota(jnp.int32, (tok, window), 0) + grp * tok
     live = (column <= row) & (column >= starts[...])
     bias = jnp.where(live, 0.0, masked_score)
-    load_kv.wait()
+    for h in range(hops):
+        rings[h].wait_recv()
+        if h + 1 < hops:
+            rings[h + 1].start()
+        sides[h].start()
+    for h in range(hops):
+        sides[h].wait_recv()
+    page_copies = send_pages(grp_count, slice(0, 1), pages, arrived, self_sem, psend, precv)
     scale = HD ** (-0.5)
     for head in range(width // HD):
         lanes = slice(head * HD, (head + 1) * HD)
-        key_head = kv[:, lanes]
-        value_head = kv[:, width + head * HD : width + (head + 1) * HD]
+        key_head = kv[:, :, lanes].reshape(window, HD)
+        value_head = kv[:, :, width + head * HD : width + (head + 1) * HD].reshape(window, HD)
         for k in range(TOPK):
             scores = lax.dot_general(
                 query[k, :, lanes], key_head, (((1,), (1,)), ((), ())),
@@ -158,22 +207,23 @@
             ) + bias
             top = jnp.max(scores, axis=-1, keepdims=True)
             weights = jnp.exp((scores - top) * scale)
-            total = jnp.sum(weights, axis=-1, keepdims=True)
+            weight_sum = jnp.sum(weights, axis=-1, keepdims=True)
             summed = jnp.dot(
                 weights.astype(jnp.bfloat16), value_head, preferred_element_type=jnp.float32
             )
-            att[k, :, lanes] = summed / total
-    info = meta[...].astype(jnp.float32)
+            att[k, :, lanes] = summed / weight_sum
     for e in range(E_ATT):
         mix = None
         for k in range(TOPK):
-            gate = jnp.where(info[:, k : k + 1] == float(e), info[:, TOPK + k : TOPK + k + 1], 0.0)
+            at = first + k
+            gate = jnp.where(
+                ids[:, at : at + 1] == float(e), ids[:, at + TOPK : at + TOPK + 1], 0.0
+            )
             term = gate * att[k]
             mix = term if mix is None else mix + term
         mixed[:, e * width : (e + 1) * width] = mix.astype(jnp.bfloat16)
     for load in load_w:
         load.wait()
-    pl.semaphore_wait(barrier, tp_count - 1)
     copies = []
     for j in list(range(1, tp_count)) + [0]:
         peer = (tp + j) % tp_count
@@ -194,14 +244,18 @@
         copy.wait()
         result = result + incoming[j].astype(jnp.float32)
     middle[...] = result.astype(jnp.bfloat16)
+    for copy in rings + sides:
+        copy.wait_send()
+    for copy in table_copies + page_copies:
+        copy.wait()
 
 
 def expert_kernel(
     tp_count, grp_count, cap, step_blocks,
-    mid_all, select, mid, mix, gain, w_gate, w_up, w_down, pages,
+    select, mid, mix, gain, w_gate, w_up, w_down, pages,
     out, arrived,
-    wg, wu, wd, gathered, xn, rs_own, rs_out, rs_in, ret_out, ret_in,
-    wsem, self_sem, psend, precv, asend, arecv, rsend, rrecv, tsend, trecv,
+    wg, wu, wd, picked, gathered, xn, rs_own, rs_out, rs_in, ret_out, ret_in,
+    wsem, self_sem, psend, precv, dsend, drecv, asend, arecv, rsend, rrecv, tsend, trecv,
 ):
     tp = lax.axis_index("tp")
     grp = lax.axis_index("grp")
@@ -221,17 +275,27 @@
         pl.semaphore_signal(
             barrier, inc=1, device_id={"grp": (grp + j) % grp_count}, device_id_type=MESH
         )
-    self_copy = pltpu.make_async_copy(pages.at[grp], arrived.at[grp], self_sem.at[0])
-    self_copy.start()
-
+    per_owner = grp_count // E_MLP
     step_rows = step_blocks * cap
     steps = grp_count // step_blocks
 
-    def pick(step):
-        for i in range(step * step_blocks, (step + 1) * step_blocks):
-            block = (grp + 1 + i) % grp_count
-            rows = jnp.dot(select[block], mid_all[block], preferred_element_type=jnp.float32)
-            gathered[tp, i * cap : (i + 1) * cap, :] = rows.astype(jnp.bfloat16)
+    picked_rows = None
+    for e in range(E_MLP):
+        picked_rows = jnp.dot(
+            select[e * cap : (e + 1) * cap, :], mid[...], preferred_element_type=jnp.float32
+        )
+        picked[e] = picked_rows.astype(jnp.bfloat16)
+    gathered[tp, 0:cap, :] = picked[grp // per_owner]
+    pl.semaphore_wait(barrier, tp_count - 1 + grp_count - 1)
+    dispatch = []
+    for i in range(1, grp_count):
+        peer = (grp + grp_count - i) % grp_count
+        copy = pltpu.make_async_remote_copy(
+            picked.at[peer // per_owner], gathered.at[tp, pl.ds(i * cap, cap)],
+            dsend.at[i - 1], drecv.at[i - 1], {"grp": peer}, MESH,
+        )
+        copy.start()
+        dispatch.append(copy)
 
     ag = []
 
@@ -247,21 +311,15 @@
             copy.start()
             ag[step].append(copy)
 
-    pick(0)
-    pl.semaphore_wait(barrier, tp_count - 1 + grp_count - 1)
-    spread(0)
-    page_copies = []
-    for j in range(1, grp_count):
-        peer = (grp + j) % grp_count
-        copy = pltpu.make_async_remote_copy(
-            pages.at[peer], arrived.at[grp], psend.at[j - 1], precv.at[j - 1],
-            {"grp": peer}, MESH,
-        )
-        copy.start()
-        page_copies.append(copy)
-    for step in range(1, steps):
-        pick(step)
+    for step in range(steps):
+        for i in range(step * step_blocks, (step + 1) * step_blocks):
+            if i:
+                dispatch[i - 1].wait_recv()
         spread(step)
+        if step == 0:
+            page_copies = send_pages(
+                grp_count, slice(1, None), pages, arrived, self_sem, psend, precv
+            ) if pages.shape[1] > 1 else []
     for load in loads:
         load.wait()
 
@@ -278,13 +336,13 @@
         for i in range(step * step_blocks, (step + 1) * step_blocks):
             part = slice(i * cap, (i + 1) * cap)
             mine = pl.ds(pl.multiple_of(grp * cap, cap), cap)
-            if i == grp_count - 1:
+            if i == 0:
                 ret_in[mine, :] = ret_out[part, :]
             else:
                 copy = pltpu.make_async_remote_copy(
                     ret_out.at[pl.ds(i * cap, cap)], ret_in.at[mine],
-                    tsend.at[i], trecv.at[i],
-                    {"grp": (grp + 1 + i) % grp_count}, MESH,
+                    tsend.at[i - 1], trecv.at[i - 1],
+                    {"grp": (grp + i) % grp_count}, MESH,
                 )
                 copy.start()
                 ret.append(copy)
@@ -331,26 +389,53 @@
     give_back(steps - 1)
     for copy in ret:
         copy.wait()
+    for copy in dispatch:
+        copy.wait_send()
     for group in ag + rs:
         for copy in group:
             copy.wait_send()
     out[...] = (
         mid[...].astype(jnp.float32)
-        + jnp.dot(mix[...], ret_in[...], preferred_element_type=jnp.float32)
+        + lax.dot_general(
+            mix[...], ret_in[...], (((0,), (0,)), ((), ())), preferred_element_type=jnp.float32
+        )
     ).astype(jnp.bfloat16)
-    self_copy.wait()
     for copy in page_copies:
         copy.wait()
 
 
-def pick_pages_kernel(order, pages, picked, sem):
+def pick_pages_kernel(order, pages, picked, held, isem, osem):
     count = pages.shape[0]
-    copies = [
-        pltpu.make_async_copy(pages.at[order[i]], picked.at[i], sem.at[i]) for i in range(count)
+    reads = [
+        pltpu.make_async_copy(pages.at[order[i]], held.at[i], isem.at[i]) for i in range(count)
     ]
-    for copy in copies:
+    writes = [pltpu.make_async_copy(held.at[i], picked.at[i], osem.at[i]) for i in range(count)]
+    for copy in reads:
         copy.start()
-    for copy in copies:
+    for read, write in zip(reads, writes):
+        read.wait()
+        write.start()
+    for copy in writes:
+        copy.wait()
+
+
+def place_pages_kernel(slot_of, *refs):
+    parts, (placed, held, isem, osem) = refs[:-4], refs[-4:]
+    reads = []
+    for part in parts:
+        for i in range(part.shape[0]):
+            at = len(reads)
+            reads.append(pltpu.make_async_copy(part.at[i], held.at[at], isem.at[at]))
+    writes = [
+        pltpu.make_async_copy(held.at[i], placed.at[slot_of[i]], osem.at[i])
+        for i in range(len(reads))
+    ]
+    for copy in reads:
+        copy.start()
+    for read, write in zip(reads, writes):
+        read.wait()
+        write.start()
+    for copy in writes:
         copy.wait()
 
 
@@ -409,24 +494,23 @@
             att_gate,
             mlp_routes.astype(bf16),
             mlp_gate,
-            jnp.broadcast_to(page_table.astype(bf16)[None, :], (rows, pages_dev)),
         ],
         axis=1,
     )
     meta = jnp.pad(meta, ((0, 0), (0, META - meta.shape[1])))
 
-    normed, kvm, resid = pl.pallas_call(
+    normed, kvm, info, resid = pl.pallas_call(
         functools.partial(key_value_kernel, tp_count),
         out_shape=(
             sds((tok, model_width), bf16),
-            sds((tok, 2 * width + META), bf16),
+            sds((tok, 2 * width), bf16),
+            sds((tok, META), bf16),
             sds((tok, width), bf16),
         ),
         in_specs=[VM] * 5 + [ANY] * 2,
-        out_specs=(VM,) * 3,
+        out_specs=(VM,) * 4,
         scratch_shapes=[
             pltpu.VMEM((tok, model_width), bf16),
-            pltpu.VMEM((tok, META), bf16),
             pltpu.VMEM(w_key.shape, bf16),
             pltpu.VMEM(w_value.shape, bf16),
             dma((2,)),
@@ -439,74 +523,6 @@
         name="gather_key_value",
     )(stream, meta, gain_attn[None, :], cosine, sine, w_key, w_value)
 
-    kv_all = lax.all_gather(kvm, "grp", axis=0, tiled=True)
-
-    meta_block = 2 * width // META
-    query = pl.pallas_call(
-        query_kernel,
-        grid=(E_ATT,),
-        out_shape=sds((TOPK, tok, width), bf16),
-        in_specs=[
-            pl.BlockSpec((tok, model_width), lambda e: (0, 0)),
-            pl.BlockSpec((tok, META), lambda e: (0, meta_block)),
-            pl.BlockSpec((tok, HD), lambda e: (0, 0)),
-            pl.BlockSpec((tok, HD), lambda e: (0, 0)),
-            pl.BlockSpec((1, model_width, width), lambda e: (e, 0, 0)),
-        ],
-        out_specs=pl.BlockSpec((TOPK, tok, width), lambda e: (0, 0, 0)),
-        scratch_shapes=[pltpu.VMEM((TOPK, tok, width), f32)],
-        compiler_params=params(),
-        name="query",
-    )(normed, kvm, cosine, sine, w_query)
-
-    info = kvm[:, 2 * width :]
-    window = (grp_count // 2 + 1) * tok
-    middle = pl.pallas_call(
-        functools.partial(attend_kernel, tp_count, grp_count),
-        out_shape=sds((tok, width), bf16),
-        in_specs=[VM] * 4 + [ANY] * 2,
-        out_specs=VM,
-        scratch_shapes=[
-            pltpu.VMEM((window, 2 * width), bf16),
-            pltpu.VMEM((E_ATT * width, model_width), bf16),
-            pltpu.VMEM((TOPK, tok, width), f32),
-            pltpu.VMEM((tok, E_ATT * width), bf16),
-            pltpu.VMEM((tp_count - 1, tok, width), bf16),
-            pltpu.VMEM((tp_count - 1, tok, width), bf16),
-            dma((1,)),
-            dma((E_ATT,)),
-            dma((tp_count - 1,)),
-            dma((tp_count - 1,)),
-        ],
-        compiler_params=params(2),
-        name="attend",
-    )(query, starts, info, resid, kv_all, w_output)
-
-    mid_all = lax.all_gather(middle, "grp", axis=0, tiled=False)
-
-    capacity = tok * TOPK * 5 // (E_MLP * 4)
-    per_owner = grp_count // E_MLP
-    my_expert = (grp_index // per_owner).astype(f32)
-    meta_all = kv_all[:, 2 * width :].reshape(grp_count, tok, META)
-    lower = jnp.arange(tok)[:, None] < jnp.arange(tok)[None, :]
-    lower = lower.astype(bf16)
-    hit = jnp.any(meta_all[:, :, 4:6].astype(f32) == my_expert, axis=2)
-    rank = jnp.dot(hit.astype(bf16), lower, preferred_element_type=f32).astype(jnp.int32)
-    slot_ids = jnp.arange(capacity, dtype=jnp.int32)
-    select = (
-        hit[:, None, :] & (rank[:, None, :] == slot_ids[None, :, None])
-    ).astype(bf16)
-    own_ids = info[:, 4:6].astype(jnp.int32)
-    own_gate = info[:, 6:8].astype(f32)
-    owner_expert = jnp.arange(grp_count, dtype=jnp.int32) // per_owner
-    own_hot = own_ids[:, :, None] == owner_expert[None, None, :]
-    own_weight = jnp.sum(jnp.where(own_hot, own_gate[:, :, None], 0.0), axis=1)
-    own_hit = jnp.any(own_hot, axis=1)
-    own_rank = jnp.dot(lower.T, own_hit.astype(bf16), preferred_element_type=f32).astype(jnp.int32)
-    mix = jnp.where(
-        own_rank[:, :, None] == slot_ids[None, None, :], own_weight[:, :, None], 0.0
-    ).astype(bf16).reshape(tok, grp_count * capacity)
-
     page_len = tok // pages_dev
     pair_pages = pages_dev // grp_count
     page_blocks = cache_in.reshape((pages_dev, page_len) + cache_in.shape[1:])
@@ -516,33 +532,97 @@
     page_order = jnp.sum(
         jnp.where(place[None, :] == page_ids[:, None], page_ids[None, :], 0), axis=1
     )
-    move_pages = pl.pallas_call(
+    page_sends = pl.pallas_call(
         pick_pages_kernel,
         out_shape=sds(page_blocks.shape, bf16),
         in_specs=[pl.BlockSpec(memory_space=pltpu.SMEM), ANY],
         out_specs=ANY,
-        scratch_shapes=[dma((pages_dev,))],
-        compiler_params=pltpu.CompilerParams(),
+        scratch_shapes=[
+            pltpu.VMEM(page_blocks.shape, bf16),
+            dma((pages_dev,)),
+            dma((pages_dev,)),
+        ],
+        compiler_params=params(),
         name="pick_pages",
-    )
-    page_sends = move_pages(page_order, page_blocks).reshape(
+    )(page_order, page_blocks).reshape(
         (grp_count, pair_pages) + page_blocks.shape[1:]
     )
 
+    window = (grp_count // 2 + 1) * tok
+    early_shape = (grp_count, 1) + page_blocks.shape[1:]
+    reach = grp_count // 2
+    peers = tp_count - 1
+    table = jnp.broadcast_to(jnp.pad(page_table, (0, META - pages_dev))[None, :], (8, META))
+    middle, early_pages, tables = pl.pallas_call(
+        functools.partial(attend_kernel, tp_count, grp_count, 0),
+        out_shape=(
+            sds((tok, width), bf16),
+            sds(early_shape, bf16),
+            sds((grp_count, 8, META), jnp.int32),
+        ),
+        in_specs=[VM] * 8 + [ANY] * 3,
+        out_specs=(VM, ANY, VM),
+        scratch_shapes=[
+            pltpu.VMEM(w_query.shape, bf16),
+            pltpu.VMEM((E_ATT * width, model_width), bf16),
+            pltpu.VMEM((reach + 1, tok, 2 * width), bf16),
+            pltpu.VMEM((TOPK, tok, width), f32),
+            pltpu.VMEM((TOPK, tok, width), bf16),
+            pltpu.VMEM((TOPK, tok, width), f32),
+            pltpu.VMEM((tok, E_ATT * width), bf16),
+            pltpu.VMEM((peers, tok, width), bf16),
+            pltpu.VMEM((peers, tok, width), bf16),
+            dma((E_ATT,)),
+            dma((E_ATT,)),
+            dma((reach // 2,)),
+            dma((reach // 2,)),
+            dma((reach // 2,)),
+            dma((reach // 2,)),
+            dma((peers,)),
+            dma((peers,)),
+            dma((1,)),
+            dma((grp_count - 1,)),
+            dma((grp_count - 1,)),
+            dma((grp_count - 1,)),
+            dma((grp_count - 1,)),
+        ],
+        compiler_params=params(2),
+        name="attend",
+    )(normed, cosine, sine, starts, info, resid, kvm, table, w_query, w_output, page_sends)
+
+    capacity = tok * TOPK * 5 // (E_MLP * 4)
+    per_owner = grp_count // E_MLP
+    lower = (jnp.arange(tok)[:, None] < jnp.arange(tok)[None, :]).astype(bf16)
+    slot_ids = jnp.arange(capacity, dtype=jnp.int32)
+    at = 2 * TOPK
+    own_ids = info[:, at : at + TOPK].astype(jnp.int32).T
+    own_gate = info[:, at + TOPK : at + 2 * TOPK].astype(f32).T
+    expert_ids = jnp.arange(E_MLP, dtype=jnp.int32)
+    own_hot = own_ids[None, :, :] == expert_ids[:, None, None]
+    own_weight = jnp.sum(jnp.where(own_hot, own_gate[None, :, :], 0.0), axis=1)
+    own_hit = jnp.any(own_hot, axis=1)
+    own_rank = jnp.dot(own_hit.astype(bf16), lower, preferred_element_type=f32).astype(jnp.int32)
+    placed = own_hit[:, None, :] & (own_rank[:, None, :] == slot_ids[None, :, None])
+    select = placed.astype(bf16).reshape(E_MLP * capacity, tok)
+    mix = jnp.where(placed, own_weight[:, None, :], 0.0).astype(bf16)
+    mix = jnp.repeat(mix, per_owner, axis=0).reshape(grp_count * capacity, tok)
+
     hid = w_gate.shape[1]
+    late_shape = (grp_count, max(pair_pages - 1, 1)) + page_blocks.shape[1:]
     step_blocks = 2
     steps = grp_count // step_blocks
     slots = grp_count * capacity
     peers = tp_count - 1
-    hidden_out, arrived = pl.pallas_call(
+    hidden_out, late_pages = pl.pallas_call(
         functools.partial(expert_kernel, tp_count, grp_count, capacity, step_blocks),
-        out_shape=(sds((tok, width), bf16), sds(page_sends.shape, bf16)),
-        in_specs=[VM] * 5 + [ANY] * 4,
+        out_shape=(sds((tok, width), bf16), sds(late_shape, bf16)),
+        in_specs=[VM] * 4 + [ANY] * 4,
         out_specs=(VM, ANY),
         scratch_shapes=[
             pltpu.VMEM((model_width, hid), bf16),
             pltpu.VMEM((model_width, hid), bf16),
             pltpu.VMEM((hid, model_width), bf16),
+            pltpu.VMEM((E_MLP, capacity, width), bf16),
             pltpu.VMEM((tp_count, slots, width), bf16),
             pltpu.VMEM((step_blocks * capacity, model_width), bf16),
             pltpu.VMEM((slots, width), f32),
@@ -554,6 +634,8 @@
             dma((1,)),
             dma((grp_count - 1,)),
             dma((grp_count - 1,)),
+            dma((grp_count - 1,)),
+            dma((grp_count - 1,)),
             dma((steps, peers)),
             dma((steps, peers)),
             dma((steps, peers)),
@@ -563,20 +645,39 @@
         ],
         compiler_params=params(3),
         name="experts",
-    )(mid_all, select, middle, mix, gain_mlp[None, :], w_gate, w_up, w_down, page_sends)
-
-    tables = meta_all[:, 0, 8 : 8 + pages_dev].astype(jnp.int32).reshape(-1)
+    )(select, middle, mix, gain_mlp[None, :], w_gate, w_up, w_down, page_sends)
+
+    tables = tables[:, 0, :pages_dev].reshape(-1)
     here = tables // pages_dev == grp_index
     all_ids = jnp.arange(tables.shape[0], dtype=jnp.int32)
     arrival = jnp.sum(
         (here[None, :] & (all_ids[None, :] < all_ids[:, None])).astype(jnp.int32), axis=1
     )
+    source = arrival // pair_pages
+    within = arrival % pair_pages
+    arrival = jnp.where(
+        within == 0, source, grp_count + source * (pair_pages - 1) + within - 1
+    )
     local = tables % pages_dev
-    slot_source = jnp.sum(
-        jnp.where(here[None, :] & (local[None, :] == page_ids[:, None]), arrival[None, :], 0),
+    slot_of = jnp.sum(
+        jnp.where(here[None, :] & (arrival[None, :] == page_ids[:, None]), local[None, :], 0),
         axis=1,
     )
-    cache_out = move_pages(slot_source, arrived.reshape(page_blocks.shape))
+    parts = [early_pages] if pair_pages == 1 else [early_pages, late_pages]
+    parts = [part.reshape((-1,) + page_blocks.shape[1:]) for part in parts]
+    cache_out = pl.pallas_call(
+        place_pages_kernel,
+        out_shape=sds(page_blocks.shape, bf16),
+        in_specs=[pl.BlockSpec(memory_space=pltpu.SMEM)] + [ANY] * len(parts),
+        out_specs=ANY,
+        scratch_shapes=[
+            pltpu.VMEM(page_blocks.shape, bf16),
+            dma((pages_dev,)),
+            dma((pages_dev,)),
+        ],
+        compiler_params=params(),
+        name="place_pages",
+    )(slot_of, *parts)
     return (hidden_out, cache_out)
 
 

time: 331 us -> 181 us (0.55)
  Pallas kernels: 261 us -> 166 us
  waiting for transfers between devices: 38.9 us -> 0 us
  between operations: 14.2 us -> 0.76 us
    pallas_call x4 -> x3, Pallas kernels: 174 us -> 62.2 us  [the longest x1 55.7 us: on_device(): pl.pallas_call(functools.partial(attend_kernel, tp_count, grp_count, 0),...]
    all_gather x2 -> x0, waiting for transfers between devices: 38.8 us -> none  [the longest x1 38.8 us: on_device(): kv_all = lax.all_gather(kvm, 'grp', axis=0, tiled=True)]
    pallas_call x1, Pallas kernels: 67.2 us -> 83 us  [on_device(): pl.pallas_call(functools.partial(expert_kernel, tp_count, grp_count, capa...]
  transfers between devices with their start and end apart: 2 -> 0, of which waited for: 1 -> 0; matrix products, arithmetic and copies ran while one was open for 3% -> 0% of each run, Pallas kernels for 23% -> 0%
where the time goes in v1:
time: 181 us; the launch traced here: 179 us
  Pallas kernels  166 us (92%)
  other arithmetic  7.95 us (4%)
  local copies, waits for them, and re-layouts  4.88 us (3%)
    pallas_call x1, Pallas kernels, on_device(): pl.pallas_call(functools.partial(expert_kernel, tp_count, grp_count, capa...  83 us
    pallas_call x1, Pallas kernels, on_device(): pl.pallas_call(functools.partial(attend_kernel, tp_count, grp_count, 0),...  55.7 us
    pallas_call x1, Pallas kernels, on_device(): pl.pallas_call(functools.partial(key_value_kernel, tp_count), out_shape=(...  20.4 us

profile of v1, /device:TPU:1, one launch (start us, length us, event | category | flops | bytes accessed | tf_op | source)
XLA Modules:
  0.0 179.3 jit_solution(16217310934084909082)
XLA Ops:
  0.6 0.0 copy-start.1
  0.7 0.8 select_reduce_fusion.4
  1.4 0.1 select_reduce_fusion.3
  1.5 0.5 fusion.4
  2.1 0.8 pad_maximum_fusion
  2.9 0.7 convert_element_type.37
  3.6 0.7 convert_element_type.38
  4.3 0.7 pad_maximum_fusion.2
  5.0 0.1 copy.36
  5.1 0.6 pad.8.meta
  5.7 20.4 %gather_key_value.1 = (bf16[256,2048]{1,0:T(8,128)(2,1)}, bf16[256,1024]{1,0:T(8,128)(2,1)}, bf16[256,128]{1,0:T(8,128)(2,1)}, bf16[256,512]{1,0:T(8,128)(2,1)}) custom-call(bf16[64,2048]{1,0:T(8,128)(2,1)} %stream.1, bf16[64,128]{1,0:T(8,128)(2,1)} %pad.8.meta, f32[1,2048]{1,0:T(1,128)} %bitcast.36, f32[256,128]{1,0:T(8,128)} %get-tuple-element.25.cosine, ...), custom_call_target="tpu_custom_call" | custom-call | tf_op jit(solution)/shard_map/gather_key_value/pallas_call | solution.py:502
  26.1 0.8 copy.38.starts
  26.9 0.0 copy-done.1
  26.9 0.2 convert_reduce_fusion.1
  27.1 0.7 select_reduce_fusion.2.order
  27.8 3.2 %pick_pages.1 = bf16[16,16,4,2,4,128]{5,4,3,2,1,0:T(4,128)(2,1)} custom-call(s32[16]{0:T(128)} %select_reduce_fusion.2.order, bf16[16,16,4,2,4,128]{5,4,3,2,1,0:T(4,128)(2,1)} %bitcast.32), custom_call_target="tpu_custom_call" | custom-call | tf_op jit(solution)/shard_map/pick_pages/pallas_call | solution.py:535
  31.0 0.6 broadcast_in_dim.78.table
  31.6 55.7 %attend.1 = (bf16[256,512]{1,0:T(8,128)(2,1)}, bf16[8,1,16,4,2,4,128]{6,5,4,3,2,1,0:T(4,128)(2,1)}, s32[8,8,128]{2,1,0:T(8,128)}) custom-call(bf16[256,2048]{1,0:T(8,128)(2,1)} %get-tuple-element.12.normed, f32[256,128]{1,0:T(8,128)} %get-tuple-element.25.cosine, f32[256,128]{1,0:T(8,128)} %get-tuple-element.26.sine, s32[256,1]{1,0:T(8,128)} %copy.38.starts, ...), custom_call_target="tpu_custom_call" | custom-call | tf_op jit(solution)/shard_map/attend/pallas_call | solution.py:556
  87.4 0.8 slice_reduce_fusion
  88.2 0.1 reshape_squeeze.3
  88.2 0.1 convert_reduce_fusion
  88.4 0.6 select_reduce_fusion.1.slot_of
  89.0 0.1 convert_bitcast_fusion
  89.1 0.1 copy.37
  89.2 0.1 copy.39
  89.3 0.1 convolution_convert_fusion
  89.5 0.1 eq.87
  89.6 0.9 fusion.mix
  90.5 0.9 fusion.2.select
  91.4 83.0 %experts.1 = (bf16[256,512]{1,0:T(8,128)(2,1)}, bf16[8,1,16,4,2,4,128]{6,5,4,3,2,1,0:T(4,128)(2,1)}) custom-call(bf16[640,256]{1,0:T(8,128)(2,1)} %fusion.2.select, bf16[256,512]{1,0:T(8,128)(2,1)} %get-tuple-element.15.mid, bf16[640,256]{1,0:T(8,128)(2,1)} %fusion.mix, f32[1,2048]{1,0:T(1,128)} %bitcast.37, bf16[2048,1408]{1,0:T(8,128)(2,1)} %w_gate.1, ...), custom_call_target="tpu_custom_call" | custom-call | tf_op jit(solution)/shard_map/experts/pallas_call | solution.py:616
  174.4 3.2 %place_pages.1 = bf16[16,16,4,2,4,128]{5,4,3,2,1,0:T(4,128)(2,1)} custom-call(s32[16]{0:T(128)} %select_reduce_fusion.1.slot_of, bf16[8,16,4,2,4,128]{5,4,3,2,1,0:T(4,128)(2,1)} %bitcast.33, bf16[8,16,4,2,4,128]{5,4,3,2,1,0:T(4,128)(2,1)} %bitcast.34), custom_call_target="tpu_custom_call" | custom-call | tf_op jit(solution)/shard_map/place_pages/pallas_call | solution.py:668
  177.6 1.7 copy.41
  (13 shorter events, 0.1 us)
Async XLA Ops:
  0.6 26.3 %copy-start.1 = (s32[16]{0:T(128)S(1)}, s32[16]{0:T(128)}, u32[]{:S(2)}) copy-start(s32[16]{0:T(128)} %param.33) | copy-start | bytes 196
  31.6 57.4 %copy-start = (bf16[256,128]{1,0:T(8,128)(2,1)S(1)}, bf16[256,128]{1,0:T(8,128)(2,1)}, u32[]{:S(2)}) copy-start(bf16[256,128]{1,0:T(8,128)(2,1)} %get-tuple-element.11.meta) | copy-start | bytes 196612

commit v2 on v1

--- a/solution.py
+++ b/solution.py
@@ -41,9 +41,9 @@
 
 
 def key_value_kernel(
-    tp_count, stream, meta, gain, cosine, sine, w_key, w_value,
+    tp_count, stream, att_routes, att_gate, mlp_routes, mlp_gate, gain, cosine, sine, w_key, w_value,
     normed, kvm, info, resid,
-    rows_all, wk, wv, wsem, send, recv, msend, mrecv,
+    rows_all, meta, wk, wv, wsem, send, recv, msend, mrecv,
 ):
     tp = lax.axis_index("tp")
     rows = stream.shape[0]
@@ -58,6 +58,11 @@
             barrier, inc=1, device_id={"tp": (tp + j) % tp_count}, device_id_type=MESH
         )
     mine = pl.ds(pl.multiple_of(tp * rows, rows), rows)
+    fields = [
+        ref[...].astype(jnp.float32) for ref in (att_routes, att_gate, mlp_routes, mlp_gate)
+    ]
+    rest = jnp.zeros((rows, META - 4 * TOPK), jnp.float32)
+    meta[...] = jnp.concatenate(fields + [rest], axis=1).astype(jnp.bfloat16)
     pl.semaphore_wait(barrier, tp_count - 1)
     copies = []
     for j in range(1, tp_count):
@@ -311,18 +316,13 @@
             copy.start()
             ag[step].append(copy)
 
-    for step in range(steps):
+    def pass_on(step):
         for i in range(step * step_blocks, (step + 1) * step_blocks):
             if i:
                 dispatch[i - 1].wait_recv()
         spread(step)
-        if step == 0:
-            page_copies = send_pages(
-                grp_count, slice(1, None), pages, arrived, self_sem, psend, precv
-            ) if pages.shape[1] > 1 else []
-    for load in loads:
-        load.wait()
-
+
+    pass_on(0)
     rs = []
     ret = []
 
@@ -347,10 +347,20 @@
                 copy.start()
                 ret.append(copy)
 
+    page_copies = []
     for step in range(steps):
         rows = slice(step * step_rows, (step + 1) * step_rows)
+        if step + 1 < steps:
+            pass_on(step + 1)
+        if step == 0 and pages.shape[1] > 1:
+            page_copies = send_pages(
+                grp_count, slice(1, None), pages, arrived, self_sem, psend, precv
+            )
         for copy in ag[step]:
             copy.wait_recv()
+        if step == 0:
+            for load in loads:
+                load.wait()
         square = None
         for s in range(tp_count):
             part = gathered[s, rows, :].astype(jnp.float32)
@@ -488,17 +498,6 @@
     cosine = jnp.concatenate([cos_half, cos_half], axis=1)
     sine = jnp.concatenate([-sin_half, sin_half], axis=1)
 
-    meta = jnp.concatenate(
-        [
-            att_routes.astype(bf16),
-            att_gate,
-            mlp_routes.astype(bf16),
-            mlp_gate,
-        ],
-        axis=1,
-    )
-    meta = jnp.pad(meta, ((0, 0), (0, META - meta.shape[1])))
-
     normed, kvm, info, resid = pl.pallas_call(
         functools.partial(key_value_kernel, tp_count),
         out_shape=(
@@ -507,10 +506,11 @@
             sds((tok, META), bf16),
             sds((tok, width), bf16),
         ),
-        in_specs=[VM] * 5 + [ANY] * 2,
+        in_specs=[VM] * 8 + [ANY] * 2,
         out_specs=(VM,) * 4,
         scratch_shapes=[
             pltpu.VMEM((tok, model_width), bf16),
+            pltpu.VMEM((rows, META), bf16),
             pltpu.VMEM(w_key.shape, bf16),
             pltpu.VMEM(w_value.shape, bf16),
             dma((2,)),
@@ -521,7 +521,7 @@
         ],
         compiler_params=params(1),
         name="gather_key_value",
-    )(stream, meta, gain_attn[None, :], cosine, sine, w_key, w_value)
+    )(stream, att_routes, att_gate, mlp_routes, mlp_gate, gain_attn[None, :], cosine, sine, w_key, w_value)
 
     page_len = tok // pages_dev
     pair_pages = pages_dev // grp_count

time: 181 us -> 178 us (0.983)
  Pallas kernels: 166 us -> 161 us
  local copies, waits for them, and re-layouts: 4.88 us -> 9.61 us
  other arithmetic: 7.95 us -> 5.91 us
    unnamed x5 -> x9, local copies, waits for them, and re-layouts: 1.68 us -> 7.12 us
    pallas_call x1, Pallas kernels: 83 us -> 78.7 us  [on_device(): pl.pallas_call(functools.partial(expert_kernel, tp_count, grp_count, capa...]
where the time goes in v2:
time: 178 us
  Pallas kernels  161 us (90%)
  local copies, waits for them, and re-layouts  9.61 us (5%)
  other arithmetic  5.91 us (3%)
    pallas_call x1, Pallas kernels, on_device(): pl.pallas_call(functools.partial(expert_kernel, tp_count, grp_count, capa...  78.7 us
    pallas_call x1, Pallas kernels, on_device(): pl.pallas_call(functools.partial(attend_kernel, tp_count, grp_count, 0),...  55.8 us
    pallas_call x1, Pallas kernels, on_device(): pl.pallas_call(functools.partial(key_value_kernel, tp_count), out_shape=(...  20.5 us
    unnamed x9, local copies, waits for them, and re-layouts  7.12 us

profile of v2, /device:TPU:1, one launch (start us, length us, event | category | flops | bytes accessed | tf_op | source)
XLA Modules:
  0.0 177.8 jit_solution(5377458334968579356)
XLA Ops:
  0.6 0.0 copy-start.1
  0.7 0.8 select_reduce_fusion.4
  1.4 0.1 select_reduce_fusion.3
  1.5 0.5 fusion.4
  2.1 0.8 pad_maximum_fusion
  2.9 1.4 copy.32.att_routes
  4.3 1.4 copy.34.mlp_routes
  5.7 1.3 copy.33.att_gate
  7.0 1.4 copy.35.mlp_gate
  8.4 20.5 %gather_key_value.1 = (bf16[256,2048]{1,0:T(8,128)(2,1)}, bf16[256,1024]{1,0:T(8,128)(2,1)}, bf16[256,128]{1,0:T(8,128)(2,1)}, bf16[256,512]{1,0:T(8,128)(2,1)}) custom-call(bf16[64,2048]{1,0:T(8,128)(2,1)} %stream.1, s32[64,2]{1,0:T(8,128)} %copy.32.att_routes, bf16[64,2]{1,0:T(8,128)(2,1)} %copy.33.att_gate, s32[64,2]{1,0:T(8,128)} %copy.34.mlp_routes, ...), custom_call_target="tpu_custom_call" | custom-call | tf_op jit(solution)/shard_map/gather_key_value/pallas_call | solution.py:501
  28.8 0.8 copy.37.starts
  29.6 0.0 copy-done.1
  29.7 0.2 convert_reduce_fusion.1
  29.8 0.7 select_reduce_fusion.2.order
  30.5 3.2 %pick_pages.1 = bf16[16,16,4,2,4,128]{5,4,3,2,1,0:T(4,128)(2,1)} custom-call(s32[16]{0:T(128)} %select_reduce_fusion.2.order, bf16[16,16,4,2,4,128]{5,4,3,2,1,0:T(4,128)(2,1)} %bitcast.32), custom_call_target="tpu_custom_call" | custom-call | tf_op jit(solution)/shard_map/pick_pages/pallas_call | solution.py:535
  33.8 0.6 broadcast_in_dim.78.table
  34.4 55.8 %attend.1 = (bf16[256,512]{1,0:T(8,128)(2,1)}, bf16[8,1,16,4,2,4,128]{6,5,4,3,2,1,0:T(4,128)(2,1)}, s32[8,8,128]{2,1,0:T(8,128)}) custom-call(bf16[256,2048]{1,0:T(8,128)(2,1)} %get-tuple-element.12.normed, f32[256,128]{1,0:T(8,128)} %get-tuple-element.25.cosine, f32[256,128]{1,0:T(8,128)} %get-tuple-element.26.sine, s32[256,1]{1,0:T(8,128)} %copy.37.starts, ...), custom_call_target="tpu_custom_call" | custom-call | tf_op jit(solution)/shard_map/attend/pallas_call | solution.py:556
  90.1 0.8 slice_reduce_fusion
  90.9 0.1 reshape_squeeze.3
  91.0 0.1 convert_reduce_fusion
  91.2 0.6 select_reduce_fusion.1.slot_of
  91.8 0.0 copy-done
  91.8 0.1 convert_bitcast_fusion
  91.9 0.1 copy.36
  92.0 0.1 copy.38
  92.1 0.1 convolution_convert_fusion
  92.3 0.1 eq.87
  92.3 0.9 fusion.mix
  93.3 0.9 fusion.2.select
  94.2 78.7 %experts.1 = (bf16[256,512]{1,0:T(8,128)(2,1)}, bf16[8,1,16,4,2,4,128]{6,5,4,3,2,1,0:T(4,128)(2,1)}) custom-call(bf16[640,256]{1,0:T(8,128)(2,1)} %fusion.2.select, bf16[256,512]{1,0:T(8,128)(2,1)} %get-tuple-element.15.mid, bf16[640,256]{1,0:T(8,128)(2,1)} %fusion.mix, f32[1,2048]{1,0:T(1,128)} %bitcast.37, bf16[2048,1408]{1,0:T(8,128)(2,1)} %w_gate.1, ...), custom_call_target="tpu_custom_call" | custom-call | tf_op jit(solution)/shard_map/experts/pallas_call | solution.py:616
  172.9 3.2 %place_pages.1 = bf16[16,16,4,2,4,128]{5,4,3,2,1,0:T(4,128)(2,1)} custom-call(s32[16]{0:T(128)} %select_reduce_fusion.1.slot_of, bf16[8,16,4,2,4,128]{5,4,3,2,1,0:T(4,128)(2,1)} %bitcast.33, bf16[8,16,4,2,4,128]{5,4,3,2,1,0:T(4,128)(2,1)} %bitcast.34), custom_call_target="tpu_custom_call" | custom-call | tf_op jit(solution)/shard_map/place_pages/pallas_call | solution.py:668
  176.1 1.7 copy.40
  (12 shorter events, 0.1 us)
Async XLA Ops:
  0.6 29.0 %copy-start.1 = (s32[16]{0:T(128)S(1)}, s32[16]{0:T(128)}, u32[]{:S(2)}) copy-start(s32[16]{0:T(128)} %param.33) | copy-start | bytes 196
  34.4 57.4 %copy-start = (bf16[256,128]{1,0:T(8,128)(2,1)S(1)}, bf16[256,128]{1,0:T(8,128)(2,1)}, u32[]{:S(2)}) copy-start(bf16[256,128]{1,0:T(8,128)(2,1)} %get-tuple-element.11.meta) | copy-start | bytes 196612
